TPU v7x, 32 devices: a whole 2x2x4 slice. The times are simulated.
32 devices in a mesh: group: 2 (over y), seq: 4 (over z), req: 2 (over x), sub: 2 (over core).
Axes of the slice: x: 2, y: 2, z: 4, core: 2. Of those that a mesh axis runs over, the one named last changes fastest.
Arguments:
- latent_codes: bfloat16 [2, 16, 2048, 512], P(None, ('group', 'req', 'sub'), 'seq'), parts along dimension 1, may hold values from -6 to 6
- latent_scales: bfloat16 [2, 16, 2048, 4], P(None, ('group', 'req', 'sub'), 'seq'), parts along dimension 1, may hold values from 0.34 to 3.5
- rope_keys: bfloat16 [2, 16, 2048, 64], P(None, ('group', 'req', 'sub'), 'seq'), parts along dimension 1, may hold values from -6 to 6
- lengths: int32 [16], P(('group', 'req', 'sub')), parts along dimension 0, may hold values from 256 to 2048, as said below
- query_latent: bfloat16 [2, 16, 4, 128, 512], P(None, ('group', 'req', 'sub'), None, 'seq'), parts along dimension 1, may hold values from -64 to 64
- query_rope: bfloat16 [2, 16, 4, 128, 64], P(None, ('group', 'req', 'sub'), None, 'seq'), parts along dimension 1, may hold values from -8 to 8
- new_latent: bfloat16 [2, 16, 4, 512], P(None, ('group', 'req', 'sub')), parts along dimension 1, may hold values from -9 to 9
- new_rope: bfloat16 [2, 16, 4, 64], P(None, ('group', 'req', 'sub')), parts along dimension 1, may hold values from -6 to 6
Outputs:
- attended: bfloat16 [2, 16, 4, 128, 512], P(None, ('group', 'req', 'sub'), None, 'seq'), parts along dimension 1
- cache_codes: bfloat16 [2, 16, 512, 4, 512], P(None, ('group', 'req', 'sub'), None, 'seq'), parts along dimension 1
- cache_scales: bfloat16 [2, 16, 512, 4, 4], P(None, ('group', 'req', 'sub'), None, 'seq'), parts along dimension 1
- cache_rope: bfloat16 [2, 16, 512, 4, 64], P(None, ('group', 'req', 'sub'), None, 'seq'), parts along dimension 1
There are 2 independent parts, one for each index of `group`. A program takes and returns all parts, laid end to end along the dimension named above; each array names one. Nothing has to cross between parts.
Inputs may be any that keep to these rules, and one draw needn't show every extreme that they name: `lengths`: one request is exactly 2048 long.
All inputs are finite; a program needn't handle non-finite values.
Results may differ from a plain program's by a relative error of at most 0.013.
Values may be sent and summed in bfloat16 or wider, within the bound.
A program may use at most 64 MiB of HBM per device.

v0:
```python
import jax
import jax.numpy as jnp
from jax import lax
from jax.sharding import PartitionSpec as P

softmax_gain = 192.0 ** (-0.5)
masked_score = -1e30


def dequantize(code_values, scale_values):
    blocks = scale_values.shape[-1]
    latent_width = code_values.shape[-1]
    shaped = code_values.astype(jnp.float32).reshape(
        code_values.shape[:-1] + (blocks, latent_width // blocks)
    )
    scaled = shaped * scale_values.astype(jnp.float32)[..., None]
    return scaled.reshape(code_values.shape).astype(jnp.bfloat16)


def shard_partial(
    lat_query, rope_query, key_rows, rope_rows, usable, new_keys, new_rope_rows, holds_new
):
    tokens_new, head_count, latent_width = lat_query.shape
    query_rows = lat_query.reshape(tokens_new * head_count, latent_width)
    query_pos = rope_query.reshape(tokens_new * head_count, rope_query.shape[-1])
    scores = jnp.dot(query_rows, key_rows.T, preferred_element_type=jnp.float32)
    scores = (
        scores + jnp.dot(query_pos, rope_rows.T, preferred_element_type=jnp.float32)
    ) * softmax_gain
    fresh_scores = jnp.dot(query_rows, new_keys.T, preferred_element_type=jnp.float32)
    fresh_scores = (
        fresh_scores + jnp.dot(query_pos, new_rope_rows.T, preferred_element_type=jnp.float32)
    ) * softmax_gain
    token_of_row = jnp.arange(tokens_new * head_count, dtype=jnp.int32) // head_count
    causal = (jnp.arange(tokens_new, dtype=jnp.int32)[None, :] <= token_of_row[:, None]) & holds_new
    scores = jnp.where(usable[None, :], scores, masked_score)
    fresh_scores = jnp.where(causal, fresh_scores, masked_score)
    group_peak = jnp.maximum(jnp.max(scores, 1), jnp.max(fresh_scores, 1)).astype(jnp.bfloat16)
    peak_float = group_peak.astype(jnp.float32)[:, None]
    weights = jnp.where(usable[None, :], jnp.exp(scores - peak_float), 0.0).astype(jnp.bfloat16)
    fresh_weights = jnp.where(causal, jnp.exp(fresh_scores - peak_float), 0.0).astype(jnp.bfloat16)
    group_total = jnp.sum(weights.astype(jnp.float32), 1) + jnp.sum(
        fresh_weights.astype(jnp.float32), 1
    )
    group_sum = jnp.dot(weights, key_rows, preferred_element_type=jnp.float32)
    group_sum = group_sum + jnp.dot(fresh_weights, new_keys, preferred_element_type=jnp.float32)
    return (
        group_sum.astype(jnp.bfloat16).reshape(tokens_new, head_count, latent_width),
        group_peak.reshape(tokens_new, head_count),
        group_total.astype(jnp.bfloat16).reshape(tokens_new, head_count),
    )


def merge_groups(pieces):
    group_sum, group_peak, group_total = pieces
    peak_float = group_peak.astype(jnp.float32)
    overall = jnp.max(peak_float, 0)
    factor = jnp.exp(peak_float - overall)
    numerator = jnp.sum(factor[..., None] * group_sum.astype(jnp.float32), 0)
    denominator = jnp.sum(factor * group_total.astype(jnp.float32), 0)
    return (numerator / denominator[..., None]).astype(jnp.bfloat16)


def per_device(
    latent_codes, latent_scales, rope_keys, lengths, query_latent, query_rope, new_latent, new_rope
):
    shard_count = lax.axis_size("seq")
    seq_index = lax.axis_index("seq")
    layer_count, request_count, span, latent_width = latent_codes.shape
    lat_query, rope_query = (
        lax.all_gather(query_latent, "seq", axis=3, tiled=True),
        lax.all_gather(query_rope, "seq", axis=3, tiled=True),
    )

    def regroup_rows(values):
        return values.reshape(
            values.shape[0], values.shape[1], span // shard_count, shard_count, values.shape[-1]
        )

    codes_moved, scales_moved, rope_moved = (
        lax.all_to_all(regroup_rows(latent_codes), "seq", split_axis=3, concat_axis=2, tiled=True),
        lax.all_to_all(regroup_rows(latent_scales), "seq", split_axis=3, concat_axis=2, tiled=True),
        lax.all_to_all(regroup_rows(rope_keys), "seq", split_axis=3, concat_axis=2, tiled=True),
    )
    offsets = jnp.arange(span, dtype=jnp.int32)
    key_rows = dequantize(latent_codes, latent_scales)
    positions = seq_index * span + offsets
    usable = positions[None, :] < lengths[:, None]
    holds_new = seq_index == 0
    per_request = jax.vmap(shard_partial, in_axes=(0, 0, 0, 0, 0, 0, 0, None))
    per_layer = jax.vmap(per_request, in_axes=(0, 0, 0, 0, None, 0, 0, None))
    group_sum, group_peak, group_total = per_layer(
        lat_query, rope_query, key_rows, rope_keys, usable, new_latent, new_rope, holds_new
    )
    attended = merge_groups(
        (
            lax.all_to_all(group_sum[None], "seq", split_axis=4, concat_axis=0, tiled=True),
            lax.all_to_all(group_peak[None], "seq", split_axis=4, concat_axis=0, tiled=True),
            lax.all_to_all(group_total[None], "seq", split_axis=4, concat_axis=0, tiled=True),
        )
    )
    return (attended, codes_moved, scales_moved, rope_moved)


def solution(mesh):
    placed = (
        P(None, ("group", "req", "sub"), "seq", None),
        P(None, ("group", "req", "sub"), "seq", None),
        P(None, ("group", "req", "sub"), "seq", None),
        P(("group", "req", "sub")),
        P(None, ("group", "req", "sub"), None, "seq", None),
        P(None, ("group", "req", "sub"), None, "seq", None),
        P(None, ("group", "req", "sub"), None, None),
        P(None, ("group", "req", "sub"), None, None),
    )
    return jax.shard_map(
        per_device,
        mesh=mesh,
        in_specs=placed,
        out_specs=(
            P(None, ("group", "req", "sub"), None, "seq", None),
            P(None, ("group", "req", "sub"), None, "seq", None),
            P(None, ("group", "req", "sub"), None, "seq", None),
            P(None, ("group", "req", "sub"), None, "seq", None),
        ),
        check_vma=False,
    )
```

profile of v0, /device:TPU:0, one launch (start us, length us, event | category | flops | bytes accessed | tf_op | source)
XLA Modules:
  0.0 215.6 jit_solution(11127280630018597931)
XLA Ops:
  7.9 1.8 reshape.126
  10.6 6.3 %all-to-all-start.4 = ((bf16[2,2,128,4,4]{2,4,1,0,3:T(4,128)(2,1)}), bf16[2,2,128,4,4]{2,4,1,0,3:T(4,128)(2,1)S(1)}, u32[]{:S(2)}, u32[]{:S(2)}) async-start(bf16[2,2,128,4,4]{2,4,1,0,3:T(4,128)(2,1)} %copy.66), calls=%async_computation.4 | async-start | bytes 32768 | tf_op jit(solution)/shard_map/all_to_all | solution.py:82
  19.2 3.4 %all-to-all-done.4 = bf16[2,2,128,4,4]{2,4,1,0,3:T(4,128)(2,1)S(1)} async-done(((bf16[2,2,128,4,4]{2,4,1,0,3:T(4,128)(2,1)}), bf16[2,2,128,4,4]{2,4,1,0,3:T(4,128)(2,1)S(1)}, u32[]{:S(2)}, u32[]{:S(2)}) %all-to-all-start.4) | async-done | bytes 16416 | tf_op jit(solution)/shard_map/all_to_all | solution.py:82
  22.5 3.4 %all-to-all-start.5 = ((bf16[2,2,128,4,64]{2,4,1,0,3:T(8,128)(2,1)}), bf16[2,2,128,4,64]{2,4,1,0,3:T(8,128)(2,1)S(1)}, u32[]{:S(2)}, u32[]{:S(2)}) async-start(bf16[2,2,128,4,64]{2,4,1,0,3:T(8,128)(2,1)} %copy.69), calls=%async_computation.5 | async-start | bytes 524288 | tf_op jit(solution)/shard_map/all_to_all | solution.py:83
  26.9 3.9 %mul.38 = f32[2,2,512,4,128]{4,3,2,1,0:T(4,128)} broadcast(f32[2,2,512,4]{3,2,1,0:T(8,128)S(1)} %copy.57), dimensions={0,1,2,3} | broadcast | bytes 4227072 | tf_op jit(solution)/shard_map/mul | solution.py:16
  30.8 5.6 %mul.39 = f32[2,2,512,512]{3,2,1,0:T(8,128)} reshape(f32[2,2,512,4,128]{4,3,2,1,0:T(4,128)} %mul.38) | data formatting | bytes 8388608 | tf_op jit(solution)/shard_map/mul | solution.py:16
  36.4 2.2 %copy.63 = bf16[2,2,512,512]{3,1,2,0:T(2,128)(2,1)S(1)} copy(bf16[2,2,512,512]{3,2,1,0:T(8,128)(2,1)S(1)} %copy-done.2) | data formatting | bytes 4194304 | tf_op args[0]
  38.6 2.0 copy.64
  40.6 1.7 all-to-all-done.5
  42.3 4.5 %all-to-all-start.3 = ((bf16[2,2,128,4,512]{4,2,1,0,3:T(8,128)(2,1)}), bf16[2,2,128,4,512]{4,2,1,0,3:T(8,128)(2,1)}, u32[]{:S(2)}, u32[]{:S(2)}) async-start(bf16[2,2,128,4,512]{4,2,1,0,3:T(8,128)(2,1)} %copy.64), calls=%async_computation.3 | async-start | bytes 4194304 | tf_op jit(solution)/shard_map/all_to_all | solution.py:81
  46.8 71.2 %all_gather.7 = bf16[2,2,4,128,64]{4,3,2,1,0:T(8,128)(2,1)S(1)} all-gather(bf16[2,2,4,32,64]{4,3,2,1,0:T(8,128)(2,1)S(1)} %copy-done.4), channel_id=1, replica_groups=mesh['group'=2,'seq'=4,'req'=2,'sub'=2] {'seq'}, dimensions={3}, use_global_device_ids=true | all-gather | bytes 327680 | tf_op jit(solution)/shard_map/all_gather | solution.py:72
  118.3 2.8 %fusion.16 = f32[2,2,512,512]{2,3,1,0:T(8,128)} fusion(bf16[2,2,512,64]{3,2,1,0:T(8,128)(2,1)S(1)} %bitcast.77, bf16[2,2,512,64]{2,3,1,0:T(8,128)(2,1)S(1)} %copy-done.3), kind=kOutput, calls=%fused_computation.39 | convolution fusion | flops 134217728 | bytes 4718592 | tf_op jit(solution)/shard_map/vmap(vmap())/dot_general | solution.py:28
  121.1 2.3 %fusion.15 = (bf16[2,2,512]{2,1,0:T(2,128)(2,1)S(1)}, f32[2,2,512,4]{2,3,1,0:T(4,128)S(1)}) fusion(f32[2,2,512,4]{2,3,1,0:T(4,128)S(1)} %fusion.17, bf16[2,2,512,512]{3,2,1,0:T(8,128)(2,1)} %bitcast.74, bf16[2,2,4,512]{3,2,1,0:T(4,128)(2,1)S(1)} %copy-done, pred[512,4]{0,1:T(4,128)(4,1)S(1)} %fusion.8), kind=kOutput, calls=%fused_computation.38 | convolution fusion | flops 8419328 | bytes 2185216 | tf_op jit(solution)/shard_map/vmap(vmap())/dot_general | solution.py:30
  123.4 5.6 %fusion.14 = (bf16[2,2,512]{2,1,0:T(2,128)(2,1)S(1)}, f32[2,2,512,512]{2,3,1,0:T(8,128)S(1)}) fusion(f32[2,2,512,512]{2,3,1,0:T(8,128)} %fusion.16, bf16[2,2,512,512]{3,2,1,0:T(8,128)(2,1)} %bitcast.75, f32[2,2,512,512]{3,2,1,0:T(8,128)} %mul.39, bf16[2,2,512,512]{3,2,1,0:T(8,128)(2,1)S(1)} %copy-done.2, pred[2,512]{1,0:T(4,128)(4,1)S(1)} %broadcast_compare_fusion), kind=kOutput, calls=%fused_computation.37 | convolution fusion | flops 1081079808 | bytes 16782336 | tf_op jit(solution)/shard_map/vmap(vmap())/dot_general | solution.py:26
  129.0 1.9 copy-done.1
  132.7 5.0 %all-to-all-start.2 = ((bf16[4,2,256]{2,1,0:T(2,128)(2,1)}), bf16[4,2,256]{2,1,0:T(2,128)(2,1)S(1)}, u32[]{:S(2)}, u32[]{:S(2)}) async-start(bf16[4,2,256]{2,1,0:T(2,128)(2,1)} %reshape.135), calls=%async_computation.2 | async-start | bytes 8192 | tf_op jit(solution)/shard_map/all_to_all | solution.py:99
  137.6 7.1 %fusion.5 = f32[2,2,512,512]{3,2,1,0:T(8,128)} fusion(f32[2,2,512,512]{2,3,1,0:T(8,128)} %copy-done.1, f32[2,2,512]{2,1,0:T(2,128)S(1)} %get-tuple-element.20, pred[2,512]{1,0:T(4,128)(4,1)S(1)} %broadcast_compare_fusion, f32[2,2,512,512]{3,2,1,0:T(8,128)} %mul.39, bf16[2,2,512,512]{3,2,1,0:T(8,128)(2,1)S(1)} %copy-done.2), kind=kOutput, calls=%fused_computation.13 | convolution fusion | flops 1080033280 | bytes 14689280 | tf_op jit(solution)/shard_map/vmap(vmap())/dot_general | solution.py:45
  145.7 5.1 %all-to-all-start = ((bf16[4,2,256]{2,1,0:T(2,128)(2,1)}), bf16[4,2,256]{2,1,0:T(2,128)(2,1)S(1)}, u32[]{:S(2)}, u32[]{:S(2)}) async-start(bf16[4,2,256]{2,1,0:T(2,128)(2,1)} %reshape.133), calls=%async_computation | async-start | bytes 8192 | tf_op jit(solution)/shard_map/all_to_all | solution.py:98
  150.8 3.0 %add_convert_fusion = bf16[2,2,512,512]{3,2,1,0:T(8,128)(2,1)S(1)} fusion(f32[2,2,512,512]{3,2,1,0:T(8,128)} %fusion.5, bf16[2,2,4,512]{3,2,1,0:T(4,128)(2,1)S(1)} %copy-done, f32[2,2,512,4]{2,3,1,0:T(4,128)S(1)} %get-tuple-element.27, f32[2,2,512]{2,1,0:T(2,128)S(1)} %get-tuple-element.20, pred[512,4]{0,1:T(4,128)(4,1)S(1)} %fusion.8), kind=kOutput, calls=%fused_computation.6 | convolution fusion | flops 10510336 | bytes 6350848 | tf_op jit(solution)/shard_map/vmap(vmap())/dot_general | solution.py:46
  153.8 3.0 %copy.61 = bf16[1,2,2,4,128,512]{5,3,2,1,0,4:T(4,128)(2,1)} copy(bf16[1,2,2,4,128,512]{5,4,3,2,1,0:T(8,128)(2,1)S(1)} %bitcast.72) | data formatting | bytes 4194304 | tf_op jit(solution)/shard_map/broadcast_in_dim;vmap(vmap())/reshape | solution.py:97
  156.8 5.1 %all-to-all-start.1 = ((bf16[1,2,2,4,128,512]{5,3,2,1,0,4:T(4,128)(2,1)}), bf16[1,2,2,4,128,512]{5,3,2,1,0,4:T(4,128)(2,1)S(1)}, u32[]{:S(2)}, u32[]{:S(2)}) async-start(bf16[1,2,2,4,128,512]{5,3,2,1,0,4:T(4,128)(2,1)} %copy.61), calls=%async_computation.1 | async-start | bytes 4194304 | tf_op jit(solution)/shard_map/all_to_all | solution.py:97
  163.2 3.1 %copy.65 = bf16[2,2,128,4,512]{4,2,3,1,0:T(8,128)(2,1)} copy(bf16[2,2,128,4,512]{4,2,1,0,3:T(8,128)(2,1)} %all-to-all-done.3) | data formatting | bytes 4194304 | tf_op jit(solution)/shard_map/all_to_all | solution.py:81
  167.4 38.4 %all-to-all-done.1 = bf16[1,2,2,4,128,512]{5,3,2,1,0,4:T(4,128)(2,1)S(1)} async-done(((bf16[1,2,2,4,128,512]{5,3,2,1,0,4:T(4,128)(2,1)}), bf16[1,2,2,4,128,512]{5,3,2,1,0,4:T(4,128)(2,1)S(1)}, u32[]{:S(2)}, u32[]{:S(2)}) %all-to-all-start.1) | async-done | bytes 2097184 | tf_op jit(solution)/shard_map/all_to_all | solution.py:97
  205.9 1.5 fusion
  (47 shorter events, 11.7 us)
Async XLA Ops:
  7.2 113.9 %copy-start = (bf16[2,2,4,512]{3,2,1,0:T(4,128)(2,1)S(1)}, bf16[2,2,4,512]{3,2,1,0:T(4,128)(2,1)}, u32[]{:S(2)}) copy-start(bf16[2,2,4,512]{3,2,1,0:T(4,128)(2,1)} %param.14) | copy-start | bytes 49156
  7.2 113.9 %all-gather.2.cloned.1.call-start = ((), (), s32[]{:S(2)}) async-start(), calls=%async_computation.6 | async-start | bytes 2621440 | tf_op jit(solution)/shard_map/all_gather | solution.py:71
  10.6 11.9 %all-to-all-start.4 = ((bf16[2,2,128,4,4]{2,4,1,0,3:T(4,128)(2,1)}), bf16[2,2,128,4,4]{2,4,1,0,3:T(4,128)(2,1)S(1)}, u32[]{:S(2)}, u32[]{:S(2)}) async-start(bf16[2,2,128,4,4]{2,4,1,0,3:T(4,128)(2,1)} %copy.66), calls=%async_computation.4 | async-start | bytes 32768 | tf_op jit(solution)/shard_map/all_to_all | solution.py:82
  22.5 19.8 %all-to-all-start.5 = ((bf16[2,2,128,4,64]{2,4,1,0,3:T(8,128)(2,1)}), bf16[2,2,128,4,64]{2,4,1,0,3:T(8,128)(2,1)S(1)}, u32[]{:S(2)}, u32[]{:S(2)}) async-start(bf16[2,2,128,4,64]{2,4,1,0,3:T(8,128)(2,1)} %copy.69), calls=%async_computation.5 | async-start | bytes 524288 | tf_op jit(solution)/shard_map/all_to_all | solution.py:83
  30.8 5.6 %copy-start.2 = (bf16[2,2,512,512]{3,2,1,0:T(8,128)(2,1)S(1)}, bf16[2,2,512,512]{3,2,1,0:T(8,128)(2,1)}, u32[]{:S(2)}) copy-start(bf16[2,2,512,512]{3,2,1,0:T(8,128)(2,1)} %param.8) | copy-start | bytes 6291460
  38.6 8.2 %copy-start.4 = (bf16[2,2,4,32,64]{4,3,2,1,0:T(8,128)(2,1)S(1)}, bf16[2,2,4,32,64]{4,3,2,1,0:T(8,128)(2,1)}, u32[]{:S(2)}) copy-start(bf16[2,2,4,32,64]{4,3,2,1,0:T(8,128)(2,1)} %param.13) | copy-start | bytes 196612
  38.6 79.4 %copy-start.6 = (s32[2]{0:T(128)S(1)}, s32[2]{0:T(128)}, u32[]{:S(2)}) copy-start(s32[2]{0:T(128)} %param.11) | copy-start | bytes 28
  38.6 79.5 %copy-start.5 = (bf16[2,2,4,64]{3,2,1,0:T(4,128)(2,1)S(1)}, bf16[2,2,4,64]{3,2,1,0:T(4,128)(2,1)}, u32[]{:S(2)}) copy-start(bf16[2,2,4,64]{3,2,1,0:T(4,128)(2,1)} %param.15) | copy-start | bytes 6148
  38.6 79.7 %copy-start.3 = (bf16[2,2,512,64]{2,3,1,0:T(8,128)(2,1)S(1)}, bf16[2,2,512,64]{2,3,1,0:T(8,128)(2,1)}, u32[]{:S(2)}) copy-start(bf16[2,2,512,64]{2,3,1,0:T(8,128)(2,1)} %param.10) | copy-start | bytes 786436
  42.3 90.3 %all-to-all-start.3 = ((bf16[2,2,128,4,512]{4,2,1,0,3:T(8,128)(2,1)}), bf16[2,2,128,4,512]{4,2,1,0,3:T(8,128)(2,1)}, u32[]{:S(2)}, u32[]{:S(2)}) async-start(bf16[2,2,128,4,512]{4,2,1,0,3:T(8,128)(2,1)} %copy.64), calls=%async_computation.3 | async-start | bytes 4194304 | tf_op jit(solution)/shard_map/all_to_all | solution.py:81
  128.9 2.0 copy-start.1
  132.7 13.1 %all-to-all-start.2 = ((bf16[4,2,256]{2,1,0:T(2,128)(2,1)}), bf16[4,2,256]{2,1,0:T(2,128)(2,1)S(1)}, u32[]{:S(2)}, u32[]{:S(2)}) async-start(bf16[4,2,256]{2,1,0:T(2,128)(2,1)} %reshape.135), calls=%async_computation.2 | async-start | bytes 8192 | tf_op jit(solution)/shard_map/all_to_all | solution.py:99
  145.7 11.0 %all-to-all-start = ((bf16[4,2,256]{2,1,0:T(2,128)(2,1)}), bf16[4,2,256]{2,1,0:T(2,128)(2,1)S(1)}, u32[]{:S(2)}, u32[]{:S(2)}) async-start(bf16[4,2,256]{2,1,0:T(2,128)(2,1)} %reshape.133), calls=%async_computation | async-start | bytes 8192 | tf_op jit(solution)/shard_map/all_to_all | solution.py:98
  156.8 49.1 %all-to-all-start.1 = ((bf16[1,2,2,4,128,512]{5,3,2,1,0,4:T(4,128)(2,1)}), bf16[1,2,2,4,128,512]{5,3,2,1,0,4:T(4,128)(2,1)S(1)}, u32[]{:S(2)}, u32[]{:S(2)}) async-start(bf16[1,2,2,4,128,512]{5,3,2,1,0,4:T(4,128)(2,1)} %copy.61), calls=%async_computation.1 | async-start | bytes 4194304 | tf_op jit(solution)/shard_map/all_to_all | solution.py:97
Sparse Core Ops, SparseCore 0:
  9.6 73.4 all-gather.1
where the time goes:
time: 216 us
  blocking collectives  71.2 us (33%)
  waiting for transfers between devices  44.2 us (20%)
  local copies, waits for them, and re-layouts  32.4 us (15%)
  starting transfers between devices  29.4 us (14%)
  matrix products  20.9 us (10%)
  between operations  14.3 us (7%)
  other arithmetic  3.24 us (2%)
    all_gather x1, blocking collectives, per_device(): lax.all_gather(query_rope, 'seq', axis=3, tiled=True)  71.2 us
    all_to_all x1, waiting for transfers between devices, per_device(): lax.all_to_all(group_sum[None], 'seq', split_axis=4, concat_axis=0, tiled...  38.4 us
    mul x2, local copies, waits for them, and re-layouts, dequantize(): scaled = shaped * scale_values.astype(jnp.float32)[..., None]  9.47 us
    unnamed x22, local copies, waits for them, and re-layouts  9.29 us
    dot_general x1, matrix products, shard_partial(): group_sum = jnp.dot(weights, key_rows, preferred_element_type=jnp.float32)  7.14 us
    all_to_all x1, starting transfers between devices, per_device(): lax.all_to_all(regroup_rows(latent_scales), 'seq', split_axis=3, concat_a...  6.32 us
    reshape x4, local copies, waits for them, and re-layouts, regroup_rows(): values.reshape(values.shape[0], values.shape[1], span // shard_count, sha...  5.68 us
    dot_general x1, matrix products, shard_partial(): scores = jnp.dot(query_rows, key_rows.T, preferred_element_type=jnp.float32)  5.57 us
  transfers between devices with their start and end apart: 7, of which 3 were waited for; matrix products, arithmetic and copies ran while one was open for 24% of the time, Pallas kernels for 0%

commit v1 on v0

--- a/solution.py
+++ b/solution.py
@@ -1,3 +1,4 @@
+import functools
 import jax
 import jax.numpy as jnp
 from jax import lax
@@ -5,6 +6,29 @@
 
 softmax_gain = 192.0 ** (-0.5)
 masked_score = -1e30
+
+
+def get_types_all(x0, peer_axis, d_out, array_axis):
+    moved = lax.axis_size(peer_axis)
+    carry_out = lax.axis_index(peer_axis)
+    y1, tmp = (moved, carry_out)
+    tall = x0.shape[d_out] // y1
+    local_now = list(x0.shape)
+    local_now[d_out] = tall
+    odd = local_now[array_axis]
+    local_now[array_axis] = odd * y1
+    front = jnp.zeros(local_now, x0.dtype)
+    for num in tuple(range(y1)):
+        block_next = lax.dynamic_slice_in_dim(x0, (tmp ^ num) * tall, tall, axis=d_out)
+        if num:
+            block_next = lax.ppermute(block_next, peer_axis, perm=[(d, d ^ num) for d in range(y1)])
+        front = lax.dynamic_update_slice_in_dim(
+            front, block_next, (tmp ^ num) * odd, axis=array_axis
+        )
+    return front
+
+
+detail_the_lots_all = functools.partial(get_types_all, peer_axis="seq", d_out=3, array_axis=2)
 
 
 def dequantize(code_values, scale_values):
@@ -79,7 +103,7 @@
 
     codes_moved, scales_moved, rope_moved = (
         lax.all_to_all(regroup_rows(latent_codes), "seq", split_axis=3, concat_axis=2, tiled=True),
-        lax.all_to_all(regroup_rows(latent_scales), "seq", split_axis=3, concat_axis=2, tiled=True),
+        detail_the_lots_all(regroup_rows(latent_scales)),
         lax.all_to_all(regroup_rows(rope_keys), "seq", split_axis=3, concat_axis=2, tiled=True),
     )
     offsets = jnp.arange(span, dtype=jnp.int32)

time: 216 us -> 261 us (1.21)
  the two profiles are of different devices: /device:TPU:0 before, /device:TPU:8 now
where the time goes in v1:
time: 261 us; the launch traced here: 260 us
  waiting for transfers between devices  80.4 us (31%)
  blocking collectives  76.8 us (29%)
  local copies, waits for them, and re-layouts  35.1 us (13%)
  starting transfers between devices  29.4 us (11%)
  matrix products  20.9 us (8%)
  between operations  14.3 us (5%)
  other arithmetic  3.25 us (1%)
    ppermute x3, waiting for transfers between devices, get_types_all(): lax.ppermute(block_next, peer_axis, perm=[(d, d ^ num) for d in range(y1)])  79.7 us
    all_gather x1, blocking collectives, per_device(): lax.all_gather(query_rope, 'seq', axis=3, tiled=True)  76.8 us
    mul x2, local copies, waits for them, and re-layouts, dequantize(): scaled = shaped * scale_values.astype(jnp.float32)[..., None]  9.47 us
    unnamed x26, local copies, waits for them, and re-layouts  9.3 us
    dot_general x1, matrix products, shard_partial(): group_sum = jnp.dot(weights, key_rows, preferred_element_type=jnp.float32)  7.16 us
    dot_general x1, matrix products, shard_partial(): scores = jnp.dot(query_rows, key_rows.T, preferred_element_type=jnp.float32)  5.57 us
    all_to_all x1, starting transfers between devices, per_device(): lax.all_to_all(regroup_rows(rope_keys), 'seq', split_axis=3, concat_axis=...  5.32 us
    all_to_all x1, starting transfers between devices, per_device(): lax.all_to_all(group_total[None], 'seq', split_axis=4, concat_axis=0, til...  5.27 us
  transfers between devices with their start and end apart: 9, of which 3 were waited for; matrix products, arithmetic and copies ran while one was open for 21% of the time, Pallas kernels for 0%

profile of v1, /device:TPU:8, one launch (start us, length us, event | category | flops | bytes accessed | tf_op | source)
XLA Modules:
  0.0 260.3 jit_solution(12269398816381501280)
XLA Ops:
  10.2 5.3 %all-to-all-start.4 = ((bf16[2,2,128,4,64]{2,4,1,0,3:T(8,128)(2,1)}), bf16[2,2,128,4,64]{2,4,1,0,3:T(8,128)(2,1)S(1)}, u32[]{:S(2)}, u32[]{:S(2)}) async-start(bf16[2,2,128,4,64]{2,4,1,0,3:T(8,128)(2,1)} %copy.81), calls=%async_computation.4 | async-start | bytes 524288 | tf_op jit(solution)/shard_map/all_to_all | solution.py:107
  16.5 3.8 %mul.50 = f32[2,2,512,4,128]{4,3,2,1,0:T(4,128)} broadcast(f32[2,2,512,4]{3,2,1,0:T(8,128)S(1)} %copy.67), dimensions={0,1,2,3} | broadcast | bytes 4227072 | tf_op jit(solution)/shard_map/mul | solution.py:40
  20.3 5.6 %mul.51 = f32[2,2,512,512]{3,2,1,0:T(8,128)} reshape(f32[2,2,512,4,128]{4,3,2,1,0:T(4,128)} %mul.50) | data formatting | bytes 8388608 | tf_op jit(solution)/shard_map/mul | solution.py:40
  25.9 2.2 copy.73
  28.1 2.0 copy.74
  30.1 5.1 %all-to-all-start.3 = ((bf16[2,2,128,4,512]{4,2,1,0,3:T(8,128)(2,1)}), bf16[2,2,128,4,512]{4,2,1,0,3:T(8,128)(2,1)}, u32[]{:S(2)}, u32[]{:S(2)}) async-start(bf16[2,2,128,4,512]{4,2,1,0,3:T(8,128)(2,1)} %copy.74), calls=%async_computation.3 | async-start | bytes 4194304 | tf_op jit(solution)/shard_map/all_to_all | solution.py:105
  35.2 76.8 %all_gather.7 = bf16[2,2,4,128,64]{4,3,2,1,0:T(8,128)(2,1)S(1)} all-gather(bf16[2,2,4,32,64]{4,3,2,1,0:T(8,128)(2,1)S(1)} %copy-done.4), channel_id=1, replica_groups=mesh['group'=2,'seq'=4,'req'=2,'sub'=2] {'seq'}, dimensions={3}, use_global_device_ids=true | all-gather | bytes 327680 | tf_op jit(solution)/shard_map/all_gather | solution.py:96
  112.4 2.8 %fusion.16 = f32[2,2,512,512]{2,3,1,0:T(8,128)} fusion(bf16[2,2,512,64]{3,2,1,0:T(8,128)(2,1)S(1)} %bitcast.70, bf16[2,2,512,64]{2,3,1,0:T(8,128)(2,1)S(1)} %copy-done.3), kind=kOutput, calls=%fused_computation.46 | convolution fusion | flops 134217728 | bytes 4718592 | tf_op jit(solution)/shard_map/vmap(vmap())/dot_general | solution.py:52
  115.2 2.3 fusion.15
  117.4 5.6 %fusion.14 = (bf16[2,2,512]{2,1,0:T(2,128)(2,1)S(1)}, f32[2,2,512,512]{2,3,1,0:T(8,128)S(1)}) fusion(f32[2,2,512,512]{2,3,1,0:T(8,128)} %fusion.16, bf16[2,2,512,512]{3,2,1,0:T(8,128)(2,1)} %bitcast.68, f32[2,2,512,512]{3,2,1,0:T(8,128)} %mul.51, bf16[2,2,512,512]{3,2,1,0:T(8,128)(2,1)S(1)} %copy-done.2, pred[2,512]{1,0:T(4,128)(4,1)S(1)} %broadcast_compare_fusion), kind=kOutput, calls=%fused_computation.44 | convolution fusion | flops 1081079808 | bytes 16782336 | tf_op jit(solution)/shard_map/vmap(vmap())/dot_general | solution.py:50
  123.1 1.9 copy-done.1
  126.7 5.3 %all-to-all-start.2 = ((bf16[4,2,256]{2,1,0:T(2,128)(2,1)}), bf16[4,2,256]{2,1,0:T(2,128)(2,1)S(1)}, u32[]{:S(2)}, u32[]{:S(2)}) async-start(bf16[4,2,256]{2,1,0:T(2,128)(2,1)} %reshape.135), calls=%async_computation.2 | async-start | bytes 8192 | tf_op jit(solution)/shard_map/all_to_all | solution.py:123
  132.0 7.2 %fusion.5 = f32[2,2,512,512]{3,2,1,0:T(8,128)} fusion(f32[2,2,512,512]{2,3,1,0:T(8,128)} %copy-done.1, f32[2,2,512]{2,1,0:T(2,128)S(1)} %get-tuple-element.20, pred[2,512]{1,0:T(4,128)(4,1)S(1)} %broadcast_compare_fusion, f32[2,2,512,512]{3,2,1,0:T(8,128)} %mul.51, bf16[2,2,512,512]{3,2,1,0:T(8,128)(2,1)S(1)} %copy-done.2), kind=kOutput, calls=%fused_computation.13 | convolution fusion | flops 1080033280 | bytes 14689280 | tf_op jit(solution)/shard_map/vmap(vmap())/dot_general | solution.py:69
  140.1 5.1 %all-to-all-start = ((bf16[4,2,256]{2,1,0:T(2,128)(2,1)}), bf16[4,2,256]{2,1,0:T(2,128)(2,1)S(1)}, u32[]{:S(2)}, u32[]{:S(2)}) async-start(bf16[4,2,256]{2,1,0:T(2,128)(2,1)} %reshape.133), calls=%async_computation | async-start | bytes 8192 | tf_op jit(solution)/shard_map/all_to_all | solution.py:122
  145.2 2.9 %add_convert_fusion = bf16[2,2,512,512]{3,2,1,0:T(8,128)(2,1)S(1)} fusion(f32[2,2,512,512]{3,2,1,0:T(8,128)} %fusion.5, bf16[2,2,4,512]{3,2,1,0:T(4,128)(2,1)S(1)} %copy-done, f32[2,2,512,4]{2,3,1,0:T(4,128)S(1)} %get-tuple-element.31, f32[2,2,512]{2,1,0:T(2,128)S(1)} %get-tuple-element.20, pred[512,4]{0,1:T(4,128)(4,1)S(1)} %fusion.8), kind=kOutput, calls=%fused_computation.6 | convolution fusion | flops 10510336 | bytes 6350848 | tf_op jit(solution)/shard_map/vmap(vmap())/dot_general | solution.py:70
  148.2 3.0 %copy.71 = bf16[1,2,2,4,128,512]{5,3,2,1,0,4:T(4,128)(2,1)} copy(bf16[1,2,2,4,128,512]{5,4,3,2,1,0:T(8,128)(2,1)S(1)} %bitcast.65) | data formatting | bytes 4194304 | tf_op jit(solution)/shard_map/broadcast_in_dim;vmap(vmap())/reshape | solution.py:121
  151.2 5.1 %all-to-all-start.1 = ((bf16[1,2,2,4,128,512]{5,3,2,1,0,4:T(4,128)(2,1)}), bf16[1,2,2,4,128,512]{5,3,2,1,0,4:T(4,128)(2,1)S(1)}, u32[]{:S(2)}, u32[]{:S(2)}) async-start(bf16[1,2,2,4,128,512]{5,3,2,1,0,4:T(4,128)(2,1)} %copy.71), calls=%async_computation.1 | async-start | bytes 4194304 | tf_op jit(solution)/shard_map/all_to_all | solution.py:121
  157.4 1.8 constant_dynamic-slice_fusion
  159.2 2.9 %collective-permute-start.1 = (bf16[2,2,128,1,4]{3,2,4,1,0:T(8,128)(2,1)}, bf16[2,2,128,1,4]{3,2,4,1,0:T(8,128)(2,1)}, u32[]{:S(2)}, u32[]{:S(2)}) collective-permute-start(bf16[2,2,128,1,4]{3,2,4,1,0:T(8,128)(2,1)} %get-tuple-element.23), channel_id=1, source_target_pairs={{0,8},{4,12},{8,0},{12,4},{1,9},{5,13},{9,1},{13,5},{2,10},{6,14},... | collective-permute-start | bytes 12296 | tf_op jit(solution)/shard_map/ppermute | solution.py:24
  163.0 40.2 %collective-permute-done = bf16[2,2,128,1,4]{3,2,4,1,0:T(8,128)(2,1)} collective-permute-done((bf16[2,2,128,1,4]{3,2,4,1,0:T(8,128)(2,1)}, bf16[2,2,128,1,4]{3,2,4,1,0:T(8,128)(2,1)}, u32[]{:S(2)}, u32[]{:S(2)}) %collective-permute-start) | collective-permute-done | bytes 4128 | tf_op jit(solution)/shard_map/ppermute | solution.py:24
  204.4 31.9 %collective-permute-done.1 = bf16[2,2,128,1,4]{3,2,4,1,0:T(8,128)(2,1)} collective-permute-done((bf16[2,2,128,1,4]{3,2,4,1,0:T(8,128)(2,1)}, bf16[2,2,128,1,4]{3,2,4,1,0:T(8,128)(2,1)}, u32[]{:S(2)}, u32[]{:S(2)}) %collective-permute-start.1) | collective-permute-done | bytes 4128 | tf_op jit(solution)/shard_map/ppermute | solution.py:24
  237.6 7.6 %collective-permute-done.2 = bf16[2,2,128,1,4]{3,2,4,1,0:T(8,128)(2,1)S(1)} collective-permute-done((bf16[2,2,128,1,4]{3,2,4,1,0:T(8,128)(2,1)}, bf16[2,2,128,1,4]{3,2,4,1,0:T(8,128)(2,1)S(1)}, u32[]{:S(2)}, u32[]{:S(2)}) %collective-permute-start.2) | collective-permute-done | bytes 4128 | tf_op jit(solution)/shard_map/ppermute | solution.py:24
  246.2 3.1 %copy.75 = bf16[2,2,128,4,512]{4,2,3,1,0:T(8,128)(2,1)} copy(bf16[2,2,128,4,512]{4,2,1,0,3:T(8,128)(2,1)} %all-to-all-done.3) | data formatting | bytes 4194304 | tf_op jit(solution)/shard_map/all_to_all | solution.py:105
  250.5 1.5 fusion
  (63 shorter events, 15.0 us)
Async XLA Ops:
  7.2 108.0 %copy-start = (bf16[2,2,4,512]{3,2,1,0:T(4,128)(2,1)S(1)}, bf16[2,2,4,512]{3,2,1,0:T(4,128)(2,1)}, u32[]{:S(2)}) copy-start(bf16[2,2,4,512]{3,2,1,0:T(4,128)(2,1)} %param.14) | copy-start | bytes 49156
  7.2 108.0 %all-gather.2.cloned.1.call-start = ((), (), s32[]{:S(2)}) async-start(), calls=%async_computation.5 | async-start | bytes 2621440 | tf_op jit(solution)/shard_map/all_gather | solution.py:95
  10.2 20.0 %all-to-all-start.4 = ((bf16[2,2,128,4,64]{2,4,1,0,3:T(8,128)(2,1)}), bf16[2,2,128,4,64]{2,4,1,0,3:T(8,128)(2,1)S(1)}, u32[]{:S(2)}, u32[]{:S(2)}) async-start(bf16[2,2,128,4,64]{2,4,1,0,3:T(8,128)(2,1)} %copy.81), calls=%async_computation.4 | async-start | bytes 524288 | tf_op jit(solution)/shard_map/all_to_all | solution.py:107
  20.3 5.6 %copy-start.2 = (bf16[2,2,512,512]{3,2,1,0:T(8,128)(2,1)S(1)}, bf16[2,2,512,512]{3,2,1,0:T(8,128)(2,1)}, u32[]{:S(2)}) copy-start(bf16[2,2,512,512]{3,2,1,0:T(8,128)(2,1)} %param.8) | copy-start | bytes 6291460
  28.1 7.1 %copy-start.4 = (bf16[2,2,4,32,64]{4,3,2,1,0:T(8,128)(2,1)S(1)}, bf16[2,2,4,32,64]{4,3,2,1,0:T(8,128)(2,1)}, u32[]{:S(2)}) copy-start(bf16[2,2,4,32,64]{4,3,2,1,0:T(8,128)(2,1)} %param.13) | copy-start | bytes 196612
  28.1 84.0 %copy-start.8 = (s32[2]{0:T(128)S(1)}, s32[2]{0:T(128)}, u32[]{:S(2)}) copy-start(s32[2]{0:T(128)} %param.11) | copy-start | bytes 28
  28.1 84.1 %copy-start.7 = (bf16[2,2,4,64]{3,2,1,0:T(4,128)(2,1)S(1)}, bf16[2,2,4,64]{3,2,1,0:T(4,128)(2,1)}, u32[]{:S(2)}) copy-start(bf16[2,2,4,64]{3,2,1,0:T(4,128)(2,1)} %param.15) | copy-start | bytes 6148
  28.1 84.3 %copy-start.3 = (bf16[2,2,512,64]{2,3,1,0:T(8,128)(2,1)S(1)}, bf16[2,2,512,64]{2,3,1,0:T(8,128)(2,1)}, u32[]{:S(2)}) copy-start(bf16[2,2,512,64]{2,3,1,0:T(8,128)(2,1)} %param.10) | copy-start | bytes 786436
  30.1 96.6 %all-to-all-start.3 = ((bf16[2,2,128,4,512]{4,2,1,0,3:T(8,128)(2,1)}), bf16[2,2,128,4,512]{4,2,1,0,3:T(8,128)(2,1)}, u32[]{:S(2)}, u32[]{:S(2)}) async-start(bf16[2,2,128,4,512]{4,2,1,0,3:T(8,128)(2,1)} %copy.74), calls=%async_computation.3 | async-start | bytes 4194304 | tf_op jit(solution)/shard_map/all_to_all | solution.py:105
  123.0 2.0 copy-start.1
  126.7 13.4 %all-to-all-start.2 = ((bf16[4,2,256]{2,1,0:T(2,128)(2,1)}), bf16[4,2,256]{2,1,0:T(2,128)(2,1)S(1)}, u32[]{:S(2)}, u32[]{:S(2)}) async-start(bf16[4,2,256]{2,1,0:T(2,128)(2,1)} %reshape.135), calls=%async_computation.2 | async-start | bytes 8192 | tf_op jit(solution)/shard_map/all_to_all | solution.py:123
  140.1 11.0 %all-to-all-start = ((bf16[4,2,256]{2,1,0:T(2,128)(2,1)}), bf16[4,2,256]{2,1,0:T(2,128)(2,1)S(1)}, u32[]{:S(2)}, u32[]{:S(2)}) async-start(bf16[4,2,256]{2,1,0:T(2,128)(2,1)} %reshape.133), calls=%async_computation | async-start | bytes 8192 | tf_op jit(solution)/shard_map/all_to_all | solution.py:122
  148.2 8.1 %copy-start.5 = (bf16[2,2,512,4]{2,3,1,0:T(4,128)(2,1)S(1)}, bf16[2,2,512,4]{2,3,1,0:T(4,128)(2,1)}, u32[]{:S(2)}) copy-start(bf16[2,2,512,4]{2,3,1,0:T(4,128)(2,1)} %param.9) | copy-start | bytes 49156
  151.2 99.3 %all-to-all-start.1 = ((bf16[1,2,2,4,128,512]{5,3,2,1,0,4:T(4,128)(2,1)}), bf16[1,2,2,4,128,512]{5,3,2,1,0,4:T(4,128)(2,1)S(1)}, u32[]{:S(2)}, u32[]{:S(2)}) async-start(bf16[1,2,2,4,128,512]{5,3,2,1,0,4:T(4,128)(2,1)} %copy.71), calls=%async_computation.1 | async-start | bytes 4194304 | tf_op jit(solution)/shard_map/all_to_all | solution.py:121
  159.2 43.9 %collective-permute-start = (bf16[2,2,128,1,4]{3,2,4,1,0:T(8,128)(2,1)}, bf16[2,2,128,1,4]{3,2,4,1,0:T(8,128)(2,1)}, u32[]{:S(2)}, u32[]{:S(2)}) collective-permute-start(bf16[2,2,128,1,4]{3,2,4,1,0:T(8,128)(2,1)} %get-tuple-element.24), channel_id=1, source_target_pairs={{0,4},{4,0},{8,12},{12,8},{1,5},{5,1},{9,13},{13,9},{2,6},{6,2},{1... | collective-permute-start | bytes 12296 | tf_op jit(solution)/shard_map/ppermute | solution.py:24
  159.2 77.1 %collective-permute-start.1 = (bf16[2,2,128,1,4]{3,2,4,1,0:T(8,128)(2,1)}, bf16[2,2,128,1,4]{3,2,4,1,0:T(8,128)(2,1)}, u32[]{:S(2)}, u32[]{:S(2)}) collective-permute-start(bf16[2,2,128,1,4]{3,2,4,1,0:T(8,128)(2,1)} %get-tuple-element.23), channel_id=1, source_target_pairs={{0,8},{4,12},{8,0},{12,4},{1,9},{5,13},{9,1},{13,5},{2,10},{6,14},... | collective-permute-start | bytes 12296 | tf_op jit(solution)/shard_map/ppermute | solution.py:24
  162.1 83.1 %collective-permute-start.2 = (bf16[2,2,128,1,4]{3,2,4,1,0:T(8,128)(2,1)}, bf16[2,2,128,1,4]{3,2,4,1,0:T(8,128)(2,1)S(1)}, u32[]{:S(2)}, u32[]{:S(2)}) collective-permute-start(bf16[2,2,128,1,4]{3,2,4,1,0:T(8,128)(2,1)} %get-tuple-element.22), channel_id=1, source_target_pairs={{0,12},{4,8},{8,4},{12,0},{1,13},{5,9},{9,5},{13,1},{2,14},{6,10},... | collective-permute-start | bytes 12296 | tf_op jit(solution)/shard_map/ppermute | solution.py:24
  245.5 6.6 %copy-start.6 = (bf16[2,2,512,1,4]{2,4,3,1,0:T(4,128)(2,1)}, bf16[2,2,512,1,4]{2,4,3,1,0:T(4,128)(2,1)S(1)}, u32[]{:S(2)}) copy-start(bf16[2,2,512,1,4]{2,4,3,1,0:T(4,128)(2,1)S(1)} %constant_dynamic-update-slice_fusion) | copy-start | bytes 49156
Sparse Core Ops, SparseCore 0:
  9.6 79.3 all-gather.1
